TPU v7x, 32 devices: a whole 2x2x4 slice. The times are simulated.
32 devices in a mesh: dp: 16 (over z, y, x), head: 2 (over core).
Axes of the slice: x: 2, y: 2, z: 4, core: 2. Of those that a mesh axis runs over, the one named last changes fastest.
Arguments:
- inputs: bfloat16 [128, 200, 768], P(('dp', 'head')), may hold values from -6 to 6
- masked: int32 [128, 200], P(('dp', 'head')), may hold values 0 or 1
- key_valid: int32 [128, 200], P('dp'), may hold values from 0 to 1, as said below
- rel_index: int32 [200, 200], replicated, may hold values from 0 to 731
- mask_token: float32 [768], replicated, may hold values from -6 to 6
- ln1_gain: float32 [768], replicated, may hold values from 0.25 to 1.75
- ln1_bias: float32 [768], replicated, may hold values from -1.75 to 1.75
- w_qkv: bfloat16 [768, 3, 768], P(None, None, 'head'), may hold values from -0.21875 to 0.21875
- qv_bias: float32 [2, 768], P(None, 'head'), may hold values from -1.75 to 1.75
- rel_table: float32 [732, 12], P(None, 'head'), may hold values from -3 to 3
- w_proj: bfloat16 [768, 768], P('head'), may hold values from -0.875 to 0.875
- proj_bias: float32 [768], replicated, may hold values from -1.75 to 1.75
- gamma1: float32 [768], replicated, may hold values from 0.5 to 1.5
- ln2_gain: float32 [768], replicated, may hold values from 0.25 to 1.75
- ln2_bias: float32 [768], replicated, may hold values from -1.75 to 1.75
- w_fc1: bfloat16 [768, 3072], P(None, ('dp', 'head')), may hold values from -0.21875 to 0.21875
- fc1_bias: bfloat16 [3072], P(('dp', 'head')), may hold values from -1.75 to 1.75
- w_fc2: bfloat16 [3072, 768], P(('dp', 'head')), may hold values from -0.109375 to 0.109375
- fc2_bias: float32 [768], replicated, may hold values from -1.75 to 1.75
- gamma2: float32 [768], replicated, may hold values from 0.5 to 1.5
- cotangent: bfloat16 [128, 200, 768], P(('dp', 'head')), may hold values from -6 to 6
Outputs:
- out: bfloat16 [128, 200, 768], P(('dp', 'head'))
- grad_input: float32 [128, 200, 768], P(('dp', 'head'))
- grad_mask_token: float32 [768], replicated
- grad_ln1_gain: float32 [768], replicated
- grad_ln1_bias: float32 [768], replicated
- grad_qkv: float32 [768, 3, 768], P(None, None, 'head')
- grad_qv_bias: float32 [2, 768], P(None, 'head')
- grad_rel_table: float32 [732, 12], P(None, 'head')
- grad_proj: float32 [768, 768], P('head')
- grad_proj_bias: float32 [768], replicated
- grad_gamma1: float32 [768], replicated
- grad_ln2_gain: float32 [768], replicated
- grad_ln2_bias: float32 [768], replicated
- grad_fc1: float32 [768, 3072], P(None, ('dp', 'head'))
- grad_fc1_bias: float32 [3072], P(('dp', 'head'))
- grad_fc2: float32 [3072, 768], P(('dp', 'head'))
- grad_fc2_bias: float32 [768], replicated
- grad_gamma2: float32 [768], replicated
Inputs may be any that keep to these rules, and one draw needn't show every extreme that they name: In each image the ones of key_valid are a leading run of rows, at least 100 long.
All inputs are finite; a program needn't handle non-finite values. No bound on the sum of `masked` on one device may be relied on, other than what follows from the above.
Results may differ from a plain program's by a relative error of at most 0.012.
The roundings to bfloat16 on the way count: a program that leaves them out, or rounds other values in their place, can miss the bound.
Values may be sent and summed in bfloat16 or wider, within the bound.
A program may use at most 256 MiB of HBM per device.

v0:
```python
import jax
import jax.numpy as jnp
from jax import lax
from jax.sharding import PartitionSpec as P

MBATCH = 2
epsilon = 1e-06
root_half = 0.7071067811865476
highest = lax.Precision.HIGHEST


def layer_norm(values, scale_vec, offset_vec):
    center = values - jnp.mean(values, axis=-1, keepdims=True)
    spread = jnp.mean(center * center, axis=-1, keepdims=True)
    return center * lax.rsqrt(spread + epsilon) * scale_vec + offset_vec


def gelu_exact(values):
    return 0.5 * values * (1.0 + jax.scipy.special.erf(values * root_half))


def block_count():
    return 4


def one_hot_block(rel_index, start, stop, entry_count):
    picked = rel_index[start:stop].reshape(-1)
    entries = lax.broadcasted_iota(jnp.int32, (1, entry_count), 1)
    return (picked[:, None] == entries).astype(jnp.float32)


def table_bias(rel_table, rel_index):
    row_count = rel_index.shape[0]
    entry_count, heads_here = rel_table.shape
    pieces = block_count()
    step_rows = row_count // pieces
    parts_list = []
    for piece_index in range(pieces):
        selector = one_hot_block(
            rel_index, piece_index * step_rows, (piece_index + 1) * step_rows, entry_count
        )
        parts_list.append(
            jnp.einsum(
                "rh,nr->hn",
                rel_table,
                selector,
                precision=highest,
                preferred_element_type=jnp.float32,
            )
        )
    return jnp.concatenate(parts_list, axis=1).reshape(heads_here, row_count, row_count)


def table_grad(score_totals, rel_index, entry_count):
    row_count = rel_index.shape[0]
    pieces = block_count()
    step_rows = row_count // pieces
    width = step_rows * row_count
    total = None
    for piece_index in range(pieces):
        selector = one_hot_block(
            rel_index, piece_index * step_rows, (piece_index + 1) * step_rows, entry_count
        )
        columns = score_totals[:, piece_index * width : (piece_index + 1) * width]
        term = jnp.einsum(
            "hn,nr->rh", columns, selector, precision=highest, preferred_element_type=jnp.float32
        )
        total = term if total is None else total + term
    return total


def score_block(queries, keyset, bias_table, valid_part, score_scale, heads_here):
    count, row_count, columns = queries.shape
    shaped = (count, row_count, heads_here, columns // heads_here)
    scores = (
        jnp.einsum(
            "gqhe,gkhe->ghqk",
            queries.reshape(shaped),
            keyset.reshape(shaped),
            preferred_element_type=jnp.float32,
        )
        * score_scale
    )
    scores = scores + bias_table[None]
    return jnp.where(valid_part[:, None, None, :] > 0, scores, -1e30)


def add_nested(left, right):
    return jax.tree.map(lambda first_val, second_val: first_val + second_val, left, right)


def reduce_end(dp_part, small_part, mlp_part):
    g_qkv, g_qvb, g_table, g_proj = dp_part
    g_mask, g_ln1g, g_ln1b, g_projb, g_gamma1, g_ln2g, g_ln2b, g_fc2b, g_gamma2 = small_part
    g_fc1, g_fc1b, g_fc2 = mlp_part
    summed_dp = lax.psum((g_qkv, g_qvb, g_table, g_proj), "dp")
    summed_small = lax.psum(
        (g_mask, g_ln1g, g_ln1b, g_projb, g_gamma1, g_ln2g, g_ln2b, g_fc2b, g_gamma2),
        ("dp", "head"),
    )
    summed_mlp = (
        lax.psum_scatter(g_fc1, ("dp", "head"), scatter_dimension=1, tiled=True),
        lax.psum_scatter(g_fc1b, ("dp", "head"), scatter_dimension=0, tiled=True),
        lax.psum_scatter(g_fc2, ("dp", "head"), scatter_dimension=0, tiled=True),
    )
    return (tuple(summed_dp), tuple(summed_small), tuple(summed_mlp))


def shards(
    inputs,
    masked,
    key_valid,
    rel_index,
    mask_token,
    ln1_gain,
    ln1_bias,
    w_qkv,
    qv_bias,
    rel_table,
    w_proj,
    proj_bias,
    gamma1,
    ln2_gain,
    ln2_bias,
    w_fc1,
    fc1_bias,
    w_fc2,
    fc2_bias,
    gamma2,
    cotangent,
):
    local_images, row_count, feature_count = inputs.shape
    group_size = lax.axis_size("head")
    part_images = local_images // MBATCH
    heads_here = rel_table.shape[1]
    head_width = w_qkv.shape[2] // heads_here
    score_scale = head_width ** (-0.5)
    bias_table = table_bias(rel_table, rel_index)
    valid_split = key_valid.reshape(group_size, local_images, row_count)
    fetched = (
        lax.all_gather(w_fc1, ("dp", "head"), axis=1, tiled=True),
        lax.all_gather(fc1_bias, ("dp", "head"), axis=0, tiled=True),
        lax.all_gather(w_fc2, ("dp", "head"), axis=0, tiled=True),
    )
    stored = []
    results = []
    for micro_index in range(MBATCH):
        offset = micro_index * part_images
        chosen = masked[offset : offset + part_images].astype(jnp.float32)[..., None]
        hidden_in = (
            inputs[offset : offset + part_images].astype(jnp.float32) * (1.0 - chosen)
            + chosen * mask_token
        )
        normed_local = layer_norm(hidden_in, ln1_gain, ln1_bias).astype(jnp.bfloat16)
        normed = lax.all_gather(normed_local, "head", axis=0, tiled=True)
        valid_part = valid_split[:, offset : offset + part_images].reshape(
            group_size * part_images, row_count
        )
        projected = jnp.einsum("gtd,dce->gtce", normed, w_qkv, preferred_element_type=jnp.float32)
        queries = (projected[:, :, 0] + qv_bias[0]).astype(jnp.bfloat16)
        keyset = projected[:, :, 1].astype(jnp.bfloat16)
        valueset = (projected[:, :, 2] + qv_bias[1]).astype(jnp.bfloat16)
        scores = score_block(queries, keyset, bias_table, valid_part, score_scale, heads_here)
        row_peak = jnp.max(scores, axis=-1, keepdims=True)
        log_total = row_peak + jnp.log(jnp.sum(jnp.exp(scores - row_peak), axis=-1, keepdims=True))
        attn_weights = jnp.exp(scores - log_total).astype(jnp.bfloat16)
        count = queries.shape[0]
        shaped = (count, row_count, heads_here, head_width)
        attended = jnp.einsum(
            "ghqk,gkhe->gqhe",
            attn_weights,
            valueset.reshape(shaped),
            preferred_element_type=jnp.float32,
        )
        attended = attended.reshape(count, row_count, heads_here * head_width).astype(jnp.bfloat16)
        partial_proj = jnp.einsum(
            "gtc,cd->gtd", attended, w_proj, preferred_element_type=jnp.float32
        )
        attn_branch = (
            lax.psum_scatter(partial_proj, "head", scatter_dimension=0, tiled=True) + proj_bias
        )
        residual = hidden_in + gamma1 * attn_branch
        normed2 = layer_norm(residual, ln2_gain, ln2_bias).astype(jnp.bfloat16)
        pre_gelu = (
            jnp.einsum("gtd,df->gtf", normed2, fetched[0], preferred_element_type=jnp.float32)
            + fetched[1]
        )
        active = gelu_exact(pre_gelu).astype(jnp.bfloat16)
        branch = (
            jnp.einsum("gtf,fd->gtd", active, fetched[2], preferred_element_type=jnp.float32)
            + fc2_bias
        )
        results.append((residual + gamma2 * branch).astype(jnp.bfloat16))
        stored.append(
            (
                offset,
                chosen,
                hidden_in,
                normed,
                valid_part,
                queries,
                keyset,
                valueset,
                log_total,
                attended,
                attn_branch,
                residual,
                normed2,
                pre_gelu,
                active,
                branch,
            )
        )
    back_weights = (fetched[0], fetched[2])
    input_grads = []
    totals = None
    for micro_index in range(MBATCH):
        (
            offset,
            chosen,
            hidden_in,
            normed,
            valid_part,
            queries,
            keyset,
            valueset,
            log_total,
            attended,
            attn_branch,
            residual,
            normed2,
            pre_gelu,
            active,
            branch,
        ) = stored[micro_index]
        upstream = cotangent[offset : offset + part_images].astype(jnp.float32)
        g_gamma2 = jnp.sum(upstream * branch, axis=(0, 1))
        grad_branch = (upstream * gamma2).astype(jnp.bfloat16)
        g_fc2b = jnp.sum(grad_branch, axis=(0, 1), dtype=jnp.float32)
        g_fc2 = jnp.einsum("gtf,gtd->fd", active, grad_branch, preferred_element_type=jnp.float32)
        grad_active = jnp.einsum(
            "gtd,fd->gtf", grad_branch, back_weights[1], preferred_element_type=jnp.float32
        )
        gelu_value, gelu_back = jax.vjp(gelu_exact, pre_gelu)
        grad_pre = gelu_back(grad_active)[0].astype(jnp.bfloat16)
        g_fc1b = jnp.sum(grad_pre, axis=(0, 1), dtype=jnp.float32)
        g_fc1 = jnp.einsum("gtd,gtf->df", normed2, grad_pre, preferred_element_type=jnp.float32)
        grad_normed2 = jnp.einsum(
            "gtf,df->gtd", grad_pre, back_weights[0], preferred_element_type=jnp.float32
        )
        norm_value, norm_back = jax.vjp(layer_norm, residual, ln2_gain, ln2_bias)
        grad_res_norm, g_ln2g, g_ln2b = norm_back(grad_normed2)
        grad_residual = upstream + grad_res_norm
        g_gamma1 = jnp.sum(grad_residual * attn_branch, axis=(0, 1))
        grad_proj_rows = (grad_residual * gamma1).astype(jnp.bfloat16)
        g_projb = jnp.sum(grad_proj_rows, axis=(0, 1), dtype=jnp.float32)
        grad_proj_full = lax.all_gather(grad_proj_rows, "head", axis=0, tiled=True)
        g_proj = jnp.einsum(
            "gtc,gtd->cd", attended, grad_proj_full, preferred_element_type=jnp.float32
        )
        grad_attended = jnp.einsum(
            "gtd,cd->gtc", grad_proj_full, w_proj, preferred_element_type=jnp.float32
        ).astype(jnp.bfloat16)
        count = queries.shape[0]
        shaped = (count, row_count, heads_here, head_width)
        scores = score_block(queries, keyset, bias_table, valid_part, score_scale, heads_here)
        soft_probs = jnp.exp(scores - log_total)
        soft_low = soft_probs.astype(jnp.bfloat16)
        grad_att4 = grad_attended.reshape(shaped)
        grad_value = jnp.einsum(
            "ghqk,gqhe->gkhe", soft_low, grad_att4, preferred_element_type=jnp.float32
        ).astype(jnp.bfloat16)
        grad_probs = jnp.einsum(
            "gqhe,gkhe->ghqk",
            grad_att4,
            valueset.reshape(shaped),
            preferred_element_type=jnp.float32,
        )
        row_delta = jnp.sum(soft_probs * grad_probs, axis=-1, keepdims=True)
        grad_scores = (soft_probs * (grad_probs - row_delta)).astype(jnp.bfloat16)
        score_totals = jnp.sum(grad_scores, axis=0, dtype=jnp.float32).reshape(
            heads_here, row_count * row_count
        )
        g_table = table_grad(score_totals, rel_index, rel_table.shape[0])
        grad_query = (
            jnp.einsum(
                "ghqk,gkhe->gqhe",
                grad_scores,
                keyset.reshape(shaped),
                preferred_element_type=jnp.float32,
            )
            * score_scale
        ).astype(jnp.bfloat16)
        grad_key = (
            jnp.einsum(
                "ghqk,gqhe->gkhe",
                grad_scores,
                queries.reshape(shaped),
                preferred_element_type=jnp.float32,
            )
            * score_scale
        ).astype(jnp.bfloat16)
        flat_cols = heads_here * head_width
        grad_stack = jnp.stack(
            (
                grad_query.reshape(count, row_count, flat_cols),
                grad_key.reshape(count, row_count, flat_cols),
                grad_value.reshape(count, row_count, flat_cols),
            ),
            axis=2,
        )
        g_qkv = jnp.einsum("gtd,gtce->dce", normed, grad_stack, preferred_element_type=jnp.float32)
        g_qvb = jnp.stack(
            (
                jnp.sum(grad_stack[:, :, 0], axis=(0, 1), dtype=jnp.float32),
                jnp.sum(grad_stack[:, :, 2], axis=(0, 1), dtype=jnp.float32),
            )
        )
        grad_normed_part = jnp.einsum(
            "gtce,dce->gtd", grad_stack, w_qkv, preferred_element_type=jnp.float32
        )
        grad_normed = lax.psum_scatter(grad_normed_part, "head", scatter_dimension=0, tiled=True)
        norm_first, norm_back_first = jax.vjp(layer_norm, hidden_in, ln1_gain, ln1_bias)
        grad_hid_norm, g_ln1g, g_ln1b = norm_back_first(grad_normed)
        grad_hidden = grad_hid_norm + grad_residual
        input_grads.append(grad_hidden * (1.0 - chosen))
        g_mask = jnp.sum(grad_hidden * chosen, axis=(0, 1))
        dp_part = (g_qkv, g_qvb, g_table, g_proj)
        small_part = (g_mask, g_ln1g, g_ln1b, g_projb, g_gamma1, g_ln2g, g_ln2b, g_fc2b, g_gamma2)
        mlp_part = (g_fc1, g_fc1b, g_fc2)
        reduced_part = (dp_part, small_part, mlp_part)
        if micro_index == 0:
            totals = reduced_part
        else:
            totals = add_nested(totals, reduced_part)
    final_sums = reduce_end(totals[0], totals[1], totals[2])
    dp_sum, small_sum, mlp_sum = final_sums
    g_qkv, g_qvb, g_table, g_proj = dp_sum
    g_mask, g_ln1g, g_ln1b, g_projb, g_gamma1, g_ln2g, g_ln2b, g_fc2b, g_gamma2 = small_sum
    g_fc1, g_fc1b, g_fc2 = mlp_sum
    return (
        jnp.concatenate(results, axis=0),
        jnp.concatenate(input_grads, axis=0),
        g_mask,
        g_ln1g,
        g_ln1b,
        g_qkv,
        g_qvb,
        g_table,
        g_proj,
        g_projb,
        g_gamma1,
        g_ln2g,
        g_ln2b,
        g_fc1,
        g_fc1b,
        g_fc2,
        g_fc2b,
        g_gamma2,
    )


def solution(mesh):
    in_specs = (
        P(("dp", "head"), None, None),
        P(("dp", "head"), None),
        P("dp", None),
        P(),
        P(),
        P(),
        P(),
        P(None, None, "head"),
        P(None, "head"),
        P(None, "head"),
        P("head", None),
        P(),
        P(),
        P(),
        P(),
        P(None, ("dp", "head")),
        P(("dp", "head")),
        P(("dp", "head"), None),
        P(),
        P(),
        P(("dp", "head"), None, None),
    )
    out_specs = (
        P(("dp", "head"), None, None),
        P(("dp", "head"), None, None),
        P(),
        P(),
        P(),
        P(None, None, "head"),
        P(None, "head"),
        P(None, "head"),
        P("head", None),
        P(),
        P(),
        P(),
        P(),
        P(None, ("dp", "head")),
        P(("dp", "head")),
        P(("dp", "head"), None),
        P(),
        P(),
    )
    return jax.shard_map(shards, mesh=mesh, in_specs=in_specs, out_specs=out_specs, check_vma=False)
```

profile of v0, /device:TPU:0, one launch (start us, length us, event | category | flops | bytes accessed | tf_op | source)
XLA Modules:
  0.0 751.6 jit_solution(7338352959528180767)
XLA Ops:
  15.9 15.1 %fusion.24 = f32[6,10000]{1,0:T(8,128)} fusion(f32[732,6]{0,1:T(8,128)} %param.30, s32[10000]{0:T(1024)S(1)} %eq.32), kind=kOutput, calls=%fused_computation.28 | convolution fusion | flops 534360000 | bytes 297568 | tf_op jit(solution)/shard_map/rh,nr->hn/dot_general | solution.py:43
  31.0 13.8 %fusion.25 = f32[6,10000]{1,0:T(8,128)S(1)} fusion(f32[732,6]{0,1:T(8,128)S(1)} %copy-done.96, s32[10000]{0:T(1024)S(1)} %eq.36), kind=kOutput, calls=%fused_computation.29 | convolution fusion | flops 534360000 | bytes 297568 | tf_op jit(solution)/shard_map/rh,nr->hn/dot_general | solution.py:43
  50.1 14.4 %fusion.26 = f32[6,10000]{1,0:T(8,128)S(1)} fusion(f32[732,6]{0,1:T(8,128)} %param.30, s32[10000]{0:T(1024)S(1)} %eq.40), kind=kOutput, calls=%fused_computation.30 | convolution fusion | flops 534360000 | bytes 297568 | tf_op jit(solution)/shard_map/rh,nr->hn/dot_general | solution.py:43
  66.7 13.6 %fusion.27 = f32[6,10000]{1,0:T(8,128)S(1)} fusion(f32[732,6]{0,1:T(8,128)S(1)} %copy-done.97, s32[10000]{0:T(1024)S(1)} %eq.44), kind=kOutput, calls=%fused_computation.31 | convolution fusion | flops 534360000 | bytes 297568 | tf_op jit(solution)/shard_map/rh,nr->hn/dot_general | solution.py:43
  114.0 43.3 %all-reduce = bf16[3072]{0:T(1024)(128)(2,1)S(1)} all-reduce(bf16[3072]{0:T(1024)(128)(2,1)S(1)} %dynamic-update-slice), channel_id=1, replica_groups=mesh['dp'=16,'head'=2] {'dp','head'}, use_global_device_ids=true, to_apply=%add | all-reduce | flops 3072 | bytes 12288
  160.4 22.3 %all-gather.9.cloned.1.call-done = bf16[768,3072]{0,1:T(8,128)(2,1)} async-done(((bf16[768,96]{0,1:T(8,128)(2,1)}), bf16[768,3072]{0,1:T(8,128)(2,1)}) %all-gather.9.cloned.1.call-update) | async-done | bytes 4718608 | tf_op jit(solution)/shard_map/all_gather | solution.py:141
  182.7 7.1 fusion.42
  189.8 57.9 %all-gather.11.cloned.1.call-done = bf16[3072,768]{1,0:T(8,128)(2,1)} async-done(((bf16[96,768]{1,0:T(8,128)(2,1)}), bf16[3072,768]{1,0:T(8,128)(2,1)}) %all-gather.11.cloned.1.call-update) | async-done | bytes 4718608 | tf_op jit(solution)/shard_map/all_gather | solution.py:143
  247.7 7.2 convert_reduce_fusion.1
  262.0 7.2 all-gather.15.cloned.1.call-done
  295.9 4.7 fusion.58
  300.6 11.3 %reduce-scatter.11.cloned.1.call-done = f32[2,200,768]{2,1,0:T(8,128)} async-done(((f32[4,200,768]{2,1,0:T(8,128)}), f32[2,200,768]{2,1,0:T(8,128)}) %reduce-scatter.11.cloned.1.call-update) | async-done | bytes 1228816 | tf_op jit(solution)/shard_map/reduce_scatter | solution.py:322
  318.1 10.4 %all-gather.13.cloned.1.call-done = bf16[4,200,768]{2,1,0:T(8,128)(2,1)} async-done(((bf16[2,200,768]{2,1,0:T(8,128)(2,1)}), bf16[4,200,768]{2,1,0:T(8,128)(2,1)}) %all-gather.13.cloned.1.call-update) | async-done | bytes 1228816 | tf_op jit(solution)/shard_map/all_gather | solution.py:155
  352.7 11.1 %reduce-scatter.9.cloned.1.call-done = f32[2,200,768]{2,1,0:T(8,128)} async-done(((f32[4,200,768]{2,1,0:T(8,128)}), f32[2,200,768]{2,1,0:T(8,128)}) %reduce-scatter.9.cloned.1.call-update) | async-done | bytes 1228816 | tf_op jit(solution)/shard_map/reduce_scatter | solution.py:180
  366.0 6.2 multiply_convert_fusion.3
  372.3 4.8 convert_reduce_fusion
  387.0 10.2 %all-gather.17.cloned.1.call-done = bf16[4,200,768]{2,1,0:T(8,128)(2,1)} async-done(((bf16[2,200,768]{2,1,0:T(8,128)(2,1)}), bf16[4,200,768]{2,1,0:T(8,128)(2,1)}) %all-gather.17.cloned.1.call-update) | async-done | bytes 1228816 | tf_op jit(solution)/shard_map/all_gather | solution.py:257
  423.8 4.7 fusion.61
  443.2 4.6 fusion.120
  447.8 5.3 bitcast_add_fusion.1
  459.0 5.7 bitcast_add_fusion
  469.8 8.2 %fusion.1 = f32[732,6]{0,1:T(8,128)S(1)} fusion(s32[10000]{0:T(1024)S(1)} %copy-done.68, f32[6,40000]{1,0:T(8,128)S(1)} %reshape.279), kind=kOutput, calls=%fused_computation.2 | convolution fusion | flops 534360000 | bytes 382112 | tf_op jit(solution)/shard_map/hn,nr->rh/dot_general | solution.py:65
  478.0 8.4 %fusion.4 = f32[732,6]{0,1:T(8,128)S(1)} fusion(s32[10000]{0:T(1024)S(1)} %copy-done.70, f32[6,40000]{1,0:T(8,128)S(1)} %reshape.279), kind=kOutput, calls=%fused_computation.6 | convolution fusion | flops 534360000 | bytes 382112 | tf_op jit(solution)/shard_map/hn,nr->rh/dot_general | solution.py:65
  486.5 8.4 %fusion.7 = f32[732,6]{0,1:T(8,128)S(1)} fusion(s32[10000]{0:T(1024)S(1)} %copy-done.66, f32[6,40000]{1,0:T(8,128)S(1)} %reshape.279), kind=kOutput, calls=%fused_computation.10 | convolution fusion | flops 534360000 | bytes 382112 | tf_op jit(solution)/shard_map/hn,nr->rh/dot_general | solution.py:65
  500.6 8.2 %fusion = f32[732,6]{0,1:T(8,128)S(1)} fusion(s32[10000]{0:T(1024)S(1)} %copy-done.68, f32[6,40000]{1,0:T(8,128)S(1)} %reshape.280), kind=kOutput, calls=%fused_computation.1 | convolution fusion | flops 534360000 | bytes 382112 | tf_op jit(solution)/shard_map/hn,nr->rh/dot_general | solution.py:65
  508.8 8.6 %fusion.3 = f32[732,6]{0,1:T(8,128)S(1)} fusion(s32[10000]{0:T(1024)S(1)} %copy-done.70, f32[6,40000]{1,0:T(8,128)S(1)} %reshape.280), kind=kOutput, calls=%fused_computation.5 | convolution fusion | flops 534360000 | bytes 382112 | tf_op jit(solution)/shard_map/hn,nr->rh/dot_general | solution.py:65
  517.4 8.4 %fusion.6 = f32[732,6]{0,1:T(8,128)S(1)} fusion(s32[10000]{0:T(1024)S(1)} %copy-done.66, f32[6,40000]{1,0:T(8,128)S(1)} %reshape.280), kind=kOutput, calls=%fused_computation.9 | convolution fusion | flops 534360000 | bytes 382112 | tf_op jit(solution)/shard_map/hn,nr->rh/dot_general | solution.py:65
  525.8 8.2 %fusion.92 = f32[732,6]{0,1:T(8,128)S(1)} fusion(f32[732,6]{0,1:T(8,128)S(1)} %fusion, f32[732,6]{0,1:T(8,128)S(1)} %fusion.3, f32[732,6]{0,1:T(8,128)S(1)} %fusion.6, s32[10000]{0:T(1024)S(1)} %copy-done.64, f32[6,40000]{1,0:T(8,128)S(1)} %reshape.280), kind=kOutput, calls=%fused_computation.177 | convolution fusion | flops 534373184 | bytes 455840 | tf_op jit(solution)/shard_map/hn,nr->rh/dot_general | solution.py:65
  534.1 9.5 %fusion.89 = f32[732,6]{0,1:T(8,128)S(1)} fusion(f32[732,6]{0,1:T(8,128)S(1)} %fusion.92, f32[732,6]{0,1:T(8,128)S(1)} %fusion.1, f32[732,6]{0,1:T(8,128)S(1)} %fusion.4, f32[732,6]{0,1:T(8,128)S(1)} %fusion.7, s32[10000]{0:T(1024)S(1)} %copy-done.64, f32[6,40000]{1,0:T(8,128)} %copy-done.37), kind=kOutput, calls=%fused_computation.174 | convolution fusion | flops 534377568 | bytes 451424 | tf_op jit(solution)/shard_map/hn,nr->rh/dot_general | solution.py:65
  543.6 78.8 %all-reduce.3 = (f32[2,384]{1,0:T(2,128)}, f32[732,6]{0,1:T(8,128)}) all-reduce(f32[2,384]{1,0:T(2,128)S(1)} %maximum_add_fusion, f32[732,6]{0,1:T(8,128)S(1)} %fusion.89), channel_id=1, replica_groups=mesh['dp'=16,'head'=2] {'dp'}, use_global_device_ids=true, to_apply=%region_40.41 | all-reduce | flops 5160 | bytes 41280 | tf_op jit(solution)/shard_map/psum | solution.py:96
  629.6 39.0 %all-reduce.2 = (f32[768]{0:T(1024)}, f32[768]{0:T(1024)}, f32[768]{0:T(1024)}, f32[768]{0:T(1024)}, f32[768]{0:T(1024)}, /*index=5*/f32[768]{0:T(1024)}, f32[76...) all-reduce(f32[768]{0:T(1024)S(1)} %add.379, ...), channel_id=1, replica_groups=mesh['dp'=16,'head'=2] {'dp','head'}, use_global_device_ids=true, to_apply=%region_28.29 | all-reduce | flops 9984 | bytes 79872 | tf_op jit(solution)/shard_map/psum | solution.py:97
  672.6 65.8 %reduce-scatter.17.cloned.1.call-done = f32[96,768]{1,0:T(8,128)} async-done(((f32[3072,768]{1,0:T(8,128)}), f32[96,768]{1,0:T(8,128)}) %reduce-scatter.17.cloned.1.call-update) | async-done | bytes 294928 | tf_op jit(solution)/shard_map/reduce_scatter | solution.py:104
  (387 shorter events, 201.5 us)
Async XLA Ops:
  8.0 80.6 %copy-start = (bf16[768,3,384]{2,0,1:T(8,128)(2,1)S(1)}, bf16[768,3,384]{2,0,1:T(8,128)(2,1)}, u32[]{:S(2)}) copy-start(bf16[768,3,384]{2,0,1:T(8,128)(2,1)} %param.28) | copy-start | bytes 5308420
  8.1 80.5 %all-gather.7.cloned.1.call-start = ((), (), s32[]{:S(2)}) async-start(), calls=%async_computation.6 | async-start | bytes 1843200 | tf_op jit(solution)/shard_map/all_gather | solution.py:155
  9.0 305.5 %copy-start.54 = (f32[2,200]{1,0:T(2,128)}, f32[2,200]{1,0:T(2,128)S(1)}, u32[]{:S(2)}) copy-start(f32[2,200]{1,0:T(2,128)S(1)} %get-tuple-element.94) | copy-start | bytes 4804
  9.8 304.7 %copy-start.56 = (f32[2,200]{1,0:T(2,128)}, f32[2,200]{1,0:T(2,128)S(1)}, u32[]{:S(2)}) copy-start(f32[2,200]{1,0:T(2,128)S(1)} %get-tuple-element.92) | copy-start | bytes 4804
  11.2 303.3 %copy-start.58 = (f32[2,200]{1,0:T(2,128)}, f32[2,200]{1,0:T(2,128)S(1)}, u32[]{:S(2)}) copy-start(f32[2,200]{1,0:T(2,128)S(1)} %broadcast_multiply_fusion.5) | copy-start | bytes 4804
  12.9 301.6 %copy-start.73 = (f32[2,200]{1,0:T(2,128)}, f32[2,200]{1,0:T(2,128)S(1)}, u32[]{:S(2)}) copy-start(f32[2,200]{1,0:T(2,128)S(1)} %fusion.121) | copy-start | bytes 4804
  14.8 142.5 %reduce-scatter.7.cloned.1.call-start = ((), (), s32[]{:S(2)}) async-start(), calls=%async_computation.7 | async-start | bytes 3686400 | tf_op jit(solution)/shard_map/reduce_scatter | solution.py:180
  45.6 21.1 %copy-start.67 = (s32[10000]{0:T(1024)}, s32[10000]{0:T(1024)S(1)}, u32[]{:S(2)}) copy-start(s32[10000]{0:T(1024)S(1)} %eq.44) | copy-start | bytes 120004
  112.5 44.8 %copy-start.71 = (f32[768]{0:T(1024)S(1)}, f32[768]{0:T(1024)}, u32[]{:S(2)}) copy-start(f32[768]{0:T(1024)} %param.32) | copy-start | bytes 9220
  112.5 44.8 %copy-start.72 = (f32[768]{0:T(1024)S(1)}, f32[768]{0:T(1024)}, u32[]{:S(2)}) copy-start(f32[768]{0:T(1024)} %param.33) | copy-start | bytes 9220
  112.5 70.2 %all-gather.9.cloned.1.call-start = ((), (), s32[]{:S(2)}) async-start(), calls=%async_computation.8 | async-start | bytes 4866048 | tf_op jit(solution)/shard_map/all_gather | solution.py:141
  113.1 134.6 %all-gather.11.cloned.1.call-start = ((), (), s32[]{:S(2)}) async-start(), calls=%async_computation.9 | async-start | bytes 4866048 | tf_op jit(solution)/shard_map/all_gather | solution.py:143
  113.7 155.4 %all-gather.15.cloned.1.call-start = ((), (), s32[]{:S(2)}) async-start(), calls=%async_computation.12 | async-start | bytes 1843200 | tf_op jit(solution)/shard_map/all_gather | solution.py:257
  159.1 23.6 %copy-start.53 = (f32[768]{0:T(1024)S(1)}, f32[768]{0:T(1024)}, u32[]{:S(2)}) copy-start(f32[768]{0:T(1024)} %param.34) | copy-start | bytes 9220
  159.1 23.6 %copy-start.62 = (f32[768]{0:T(1024)S(1)}, f32[768]{0:T(1024)}, u32[]{:S(2)}) copy-start(f32[768]{0:T(1024)} %param.35) | copy-start | bytes 9220
  160.4 87.3 %copy-start.89 = (f32[768]{0:T(1024)S(1)}, f32[768]{0:T(1024)}, u32[]{:S(2)}) copy-start(f32[768]{0:T(1024)} %param.40) | copy-start | bytes 9220
  261.4 50.5 %reduce-scatter.11.cloned.1.call-start = ((), (), s32[]{:S(2)}) async-start(), calls=%async_computation.13 | async-start | bytes 3686400 | tf_op jit(solution)/shard_map/reduce_scatter | solution.py:322
  300.6 28.0 %all-gather.13.cloned.1.call-start = ((), (), s32[]{:S(2)}) async-start(), calls=%async_computation.10 | async-start | bytes 1843200 | tf_op jit(solution)/shard_map/all_gather | solution.py:155
  317.9 45.9 %reduce-scatter.9.cloned.1.call-start = ((), (), s32[]{:S(2)}) async-start(), calls=%async_computation.11 | async-start | bytes 3686400 | tf_op jit(solution)/shard_map/reduce_scatter | solution.py:180
  352.4 44.8 %all-gather.17.cloned.1.call-start = ((), (), s32[]{:S(2)}) async-start(), calls=%async_computation.14 | async-start | bytes 1843200 | tf_op jit(solution)/shard_map/all_gather | solution.py:257
  386.5 235.9 %reduce-scatter.13.cloned.1.call-start = ((), (), s32[]{:S(2)}) async-start(), calls=%async_computation.15 | async-start | bytes 3686400 | tf_op jit(solution)/shard_map/reduce_scatter | solution.py:322
  428.5 244.0 %all-reduce.7.cloned.1.call-start = ((), (), s32[]{:S(2)}) async-start(), calls=%async_computation.18 | async-start | bytes 9437184 | tf_op jit(solution)/shard_map/psum | solution.py:96
  441.9 230.6 %reduce-scatter.15.cloned.1.call-start = ((), (), s32[]{:S(2)}) async-start(), calls=%async_computation.16 | async-start | bytes 9732096 | tf_op jit(solution)/shard_map/reduce_scatter | solution.py:102
  453.2 285.2 %reduce-scatter.17.cloned.1.call-start = ((), (), s32[]{:S(2)}) async-start(), calls=%async_computation.17 | async-start | bytes 9732096 | tf_op jit(solution)/shard_map/reduce_scatter | solution.py:104
  534.0 88.4 %copy-start.18 = (f32[2,200,768]{2,1,0:T(8,128)S(1)}, f32[2,200,768]{2,1,0:T(8,128)}, u32[]{:S(2)}) copy-start(f32[2,200,768]{2,1,0:T(8,128)} %reduce-scatter.11.cloned.1.call-done) | copy-start | bytes 3686404
  534.0 88.4 %copy-start.52 = (f32[768]{0:T(1024)S(1)}, f32[768]{0:T(1024)}, u32[]{:S(2)}) copy-start(f32[768]{0:T(1024)} %param.26) | copy-start | bytes 9220
  534.0 88.4 %copy-start.55 = (f32[2,200]{1,0:T(2,128)S(1)}, f32[2,200]{1,0:T(2,128)}, u32[]{:S(2)}) copy-start(f32[2,200]{1,0:T(2,128)} %copy-done.54) | copy-start | bytes 4804
  534.1 88.4 %copy-start.57 = (f32[2,200]{1,0:T(2,128)S(1)}, f32[2,200]{1,0:T(2,128)}, u32[]{:S(2)}) copy-start(f32[2,200]{1,0:T(2,128)} %copy-done.56) | copy-start | bytes 4804
  534.1 88.4 %copy-start.59 = (f32[2,200]{1,0:T(2,128)S(1)}, f32[2,200]{1,0:T(2,128)}, u32[]{:S(2)}) copy-start(f32[2,200]{1,0:T(2,128)} %copy-done.58) | copy-start | bytes 4804
  534.1 88.4 %copy-start.61 = (f32[2,200]{1,0:T(2,128)S(1)}, f32[2,200]{1,0:T(2,128)}, u32[]{:S(2)}) copy-start(f32[2,200]{1,0:T(2,128)} %copy-done.60) | copy-start | bytes 4804
  534.1 88.4 %copy-start.74 = (f32[2,200]{1,0:T(2,128)S(1)}, f32[2,200]{1,0:T(2,128)}, u32[]{:S(2)}) copy-start(f32[2,200]{1,0:T(2,128)} %copy-done.73) | copy-start | bytes 4804
  534.1 88.4 %copy-start.80 = (f32[2,200]{1,0:T(2,128)S(1)}, f32[2,200]{1,0:T(2,128)}, u32[]{:S(2)}) copy-start(f32[2,200]{1,0:T(2,128)} %copy-done.79) | copy-start | bytes 4804
  (91 other events, 471.1 us)
Sparse Core Ops, SparseCore 0:
  14.9 11.9 all-gather.6
  112.6 12.7 reduce-scatter.6
  261.6 7.5 all-gather.14
  300.7 11.1 reduce-scatter.10
  318.0 10.5 all-gather.12
  352.5 11.1 reduce-scatter.8
  386.7 10.5 all-gather.16
  428.7 11.1 reduce-scatter.12
  453.3 144.2 reduce-scatter.14
  604.0 134.3 reduce-scatter.16
Sparse Core Ops, SparseCore 1:
  115.9 66.8 all-gather.8
  185.5 62.1 all-gather.10
  442.0 200.4 all-reduce.6
where the time goes:
time: 763 us; the launch traced here: 752 us
  matrix products  252 us (33%)
  waiting for transfers between devices  197 us (26%)
  blocking collectives  161 us (21%)
  local copies, waits for them, and re-layouts  82.8 us (11%)
  other arithmetic  39 us (5%)
  between operations  17.7 us (2%)
    psum x1, blocking collectives, reduce_end(): summed_dp = lax.psum((g_qkv, g_qvb, g_table, g_proj), 'dp')  78.8 us
    dot_general x8, matrix products, table_grad(): jnp.einsum('hn,nr->rh', columns, selector, precision=highest, preferred_e...  67.8 us
    reduce_scatter x1, waiting for transfers between devices, reduce_end(): lax.psum_scatter(g_fc2, ('dp', 'head'), scatter_dimension=0, tiled=True)  65.8 us
    all_gather x1, waiting for transfers between devices, shards(): lax.all_gather(w_fc2, ('dp', 'head'), axis=0, tiled=True)  57.9 us
    dot_general x4, matrix products, table_bias(): jnp.einsum('rh,nr->hn', rel_table, selector, precision=highest, preferred...  56.8 us
    unnamed x1, blocking collectives  43.3 us
    psum x1, blocking collectives, reduce_end(): lax.psum((g_mask, g_ln1g, g_ln1b, g_projb, g_gamma1, g_ln2g, g_ln2b, g_fc...  39 us
    unnamed x228, local copies, waits for them, and re-layouts  27.3 us
  transfers between devices with their start and end apart: 13, of which 8 were waited for; matrix products, arithmetic and copies ran while one was open for 27% of the time, Pallas kernels for 0%

commit v1 on v0

--- a/solution.py
+++ b/solution.py
@@ -95,8 +95,10 @@
     g_fc1, g_fc1b, g_fc2 = mlp_part
     summed_dp = lax.psum((g_qkv, g_qvb, g_table, g_proj), "dp")
     summed_small = lax.psum(
-        (g_mask, g_ln1g, g_ln1b, g_projb, g_gamma1, g_ln2g, g_ln2b, g_fc2b, g_gamma2),
-        ("dp", "head"),
+        lax.psum(
+            (g_mask, g_ln1g, g_ln1b, g_projb, g_gamma1, g_ln2g, g_ln2b, g_fc2b, g_gamma2), "head"
+        ),
+        "dp",
     )
     summed_mlp = (
         lax.psum_scatter(g_fc1, ("dp", "head"), scatter_dimension=1, tiled=True),

time: 763 us -> 764 us (level)
  blocking collectives: 161 us -> 169 us
    unnamed x1 -> x2, blocking collectives: 43.3 us -> 87.1 us
    psum x1, blocking collectives: 39 us -> 3.52 us  [reduce_end(): lax.psum((g_mask, g_ln1g, g_ln1b, g_projb, g_gamma1, g_ln2g, g_ln2b, g_fc...]
    reduce_scatter x1, waiting for transfers between devices: 65.8 us -> 58.1 us  [reduce_end(): lax.psum_scatter(g_fc2, ('dp', 'head'), scatter_dimension=0, tiled=True)]
    unnamed x228 -> x224, local copies, waits for them, and re-layouts: 27.3 us -> 26.6 us
where the time goes in v1:
time: 764 us; the launch traced here: 753 us
  matrix products  252 us (33%)
  waiting for transfers between devices  190 us (25%)
  blocking collectives  169 us (22%)
  local copies, waits for them, and re-layouts  82.1 us (11%)
  other arithmetic  40.3 us (5%)
  between operations  17.7 us (2%)
    unnamed x2, blocking collectives  87.1 us
    psum x1, blocking collectives, reduce_end(): lax.psum(lax.psum((g_mask, g_ln1g, g_ln1b, g_projb, g_gamma1, g_ln2g, g_l...  78.8 us
    dot_general x8, matrix products, table_grad(): jnp.einsum('hn,nr->rh', columns, selector, precision=highest, preferred_e...  67.9 us
    reduce_scatter x1, waiting for transfers between devices, reduce_end(): lax.psum_scatter(g_fc2, ('dp', 'head'), scatter_dimension=0, tiled=True)  58.1 us
    all_gather x1, waiting for transfers between devices, shards(): lax.all_gather(w_fc2, ('dp', 'head'), axis=0, tiled=True)  57.9 us
    dot_general x4, matrix products, table_bias(): jnp.einsum('rh,nr->hn', rel_table, selector, precision=highest, preferred...  56.8 us
    unnamed x224, local copies, waits for them, and re-layouts  26.6 us
    all_gather x1, waiting for transfers between devices, shards(): lax.all_gather(w_fc1, ('dp', 'head'), axis=1, tiled=True)  22.3 us
  transfers between devices with their start and end apart: 13, of which 8 were waited for; matrix products, arithmetic and copies ran while one was open for 27% of the time, Pallas kernels for 0%

profile of v1, /device:TPU:0, one launch (start us, length us, event | category | flops | bytes accessed | tf_op | source)
XLA Modules:
  0.0 752.7 jit_solution(16934211448008377493)
XLA Ops:
  15.9 15.1 %fusion.24 = f32[6,10000]{1,0:T(8,128)} fusion(f32[732,6]{0,1:T(8,128)} %param.30, s32[10000]{0:T(1024)S(1)} %eq.32), kind=kOutput, calls=%fused_computation.28 | convolution fusion | flops 534360000 | bytes 297568 | tf_op jit(solution)/shard_map/rh,nr->hn/dot_general | solution.py:43
  31.0 13.8 %fusion.25 = f32[6,10000]{1,0:T(8,128)S(1)} fusion(f32[732,6]{0,1:T(8,128)S(1)} %copy-done.94, s32[10000]{0:T(1024)S(1)} %eq.36), kind=kOutput, calls=%fused_computation.29 | convolution fusion | flops 534360000 | bytes 297568 | tf_op jit(solution)/shard_map/rh,nr->hn/dot_general | solution.py:43
  50.1 14.4 %fusion.26 = f32[6,10000]{1,0:T(8,128)S(1)} fusion(f32[732,6]{0,1:T(8,128)} %param.30, s32[10000]{0:T(1024)S(1)} %eq.40), kind=kOutput, calls=%fused_computation.30 | convolution fusion | flops 534360000 | bytes 297568 | tf_op jit(solution)/shard_map/rh,nr->hn/dot_general | solution.py:43
  66.7 13.6 %fusion.27 = f32[6,10000]{1,0:T(8,128)S(1)} fusion(f32[732,6]{0,1:T(8,128)S(1)} %copy-done.95, s32[10000]{0:T(1024)S(1)} %eq.44), kind=kOutput, calls=%fused_computation.31 | convolution fusion | flops 534360000 | bytes 297568 | tf_op jit(solution)/shard_map/rh,nr->hn/dot_general | solution.py:43
  114.0 43.2 %all-reduce = bf16[3072]{0:T(1024)(128)(2,1)S(1)} all-reduce(bf16[3072]{0:T(1024)(128)(2,1)S(1)} %dynamic-update-slice), channel_id=1, replica_groups=mesh['dp'=16,'head'=2] {'dp','head'}, use_global_device_ids=true, to_apply=%add | all-reduce | flops 3072 | bytes 12288
  160.4 22.3 %all-gather.9.cloned.1.call-done = bf16[768,3072]{0,1:T(8,128)(2,1)} async-done(((bf16[768,96]{0,1:T(8,128)(2,1)}), bf16[768,3072]{0,1:T(8,128)(2,1)}) %all-gather.9.cloned.1.call-update) | async-done | bytes 4718608 | tf_op jit(solution)/shard_map/all_gather | solution.py:143
  182.7 7.1 fusion.42
  189.8 57.9 %all-gather.11.cloned.1.call-done = bf16[3072,768]{1,0:T(8,128)(2,1)} async-done(((bf16[96,768]{1,0:T(8,128)(2,1)}), bf16[3072,768]{1,0:T(8,128)(2,1)}) %all-gather.11.cloned.1.call-update) | async-done | bytes 4718608 | tf_op jit(solution)/shard_map/all_gather | solution.py:145
  247.7 7.2 convert_reduce_fusion.1
  261.9 7.2 all-gather.15.cloned.1.call-done
  274.5 4.6 convert_reduce_fusion.6
  295.9 4.7 fusion.58
  300.6 11.3 %reduce-scatter.11.cloned.1.call-done = f32[2,200,768]{2,1,0:T(8,128)} async-done(((f32[4,200,768]{2,1,0:T(8,128)}), f32[2,200,768]{2,1,0:T(8,128)}) %reduce-scatter.11.cloned.1.call-update) | async-done | bytes 1228816 | tf_op jit(solution)/shard_map/reduce_scatter | solution.py:324
  318.1 10.4 %all-gather.13.cloned.1.call-done = bf16[4,200,768]{2,1,0:T(8,128)(2,1)} async-done(((bf16[2,200,768]{2,1,0:T(8,128)(2,1)}), bf16[4,200,768]{2,1,0:T(8,128)(2,1)}) %all-gather.13.cloned.1.call-update) | async-done | bytes 1228816 | tf_op jit(solution)/shard_map/all_gather | solution.py:157
  352.7 11.1 %reduce-scatter.9.cloned.1.call-done = f32[2,200,768]{2,1,0:T(8,128)} async-done(((f32[4,200,768]{2,1,0:T(8,128)}), f32[2,200,768]{2,1,0:T(8,128)}) %reduce-scatter.9.cloned.1.call-update) | async-done | bytes 1228816 | tf_op jit(solution)/shard_map/reduce_scatter | solution.py:182
  366.0 6.2 multiply_convert_fusion.3
  372.3 4.9 convert_reduce_fusion
  387.0 10.2 %all-gather.17.cloned.1.call-done = bf16[4,200,768]{2,1,0:T(8,128)(2,1)} async-done(((bf16[2,200,768]{2,1,0:T(8,128)(2,1)}), bf16[4,200,768]{2,1,0:T(8,128)(2,1)}) %all-gather.17.cloned.1.call-update) | async-done | bytes 1228816 | tf_op jit(solution)/shard_map/all_gather | solution.py:259
  423.8 4.7 fusion.61
  447.8 5.4 bitcast_add_fusion.1
  459.0 5.7 bitcast_add_fusion
  469.8 8.2 %fusion.1 = f32[732,6]{0,1:T(8,128)S(1)} fusion(s32[10000]{0:T(1024)S(1)} %copy-done.66, f32[6,40000]{1,0:T(8,128)S(1)} %reshape.279), kind=kOutput, calls=%fused_computation.2 | convolution fusion | flops 534360000 | bytes 382112 | tf_op jit(solution)/shard_map/hn,nr->rh/dot_general | solution.py:65
  478.0 8.4 %fusion.4 = f32[732,6]{0,1:T(8,128)S(1)} fusion(s32[10000]{0:T(1024)S(1)} %copy-done.68, f32[6,40000]{1,0:T(8,128)S(1)} %reshape.279), kind=kOutput, calls=%fused_computation.6 | convolution fusion | flops 534360000 | bytes 382112 | tf_op jit(solution)/shard_map/hn,nr->rh/dot_general | solution.py:65
  486.4 8.6 %fusion.7 = f32[732,6]{0,1:T(8,128)S(1)} fusion(s32[10000]{0:T(1024)S(1)} %copy-done.64, f32[6,40000]{1,0:T(8,128)S(1)} %reshape.279), kind=kOutput, calls=%fused_computation.10 | convolution fusion | flops 534360000 | bytes 382112 | tf_op jit(solution)/shard_map/hn,nr->rh/dot_general | solution.py:65
  495.1 43.8 %all-reduce.1 = f32[3072]{0:T(1024)S(1)} all-reduce(f32[3072]{0:T(1024)S(1)} %add.415), channel_id=7, replica_groups=mesh['dp'=16,'head'=2] {'dp','head'}, use_global_device_ids=true, to_apply=%region_67.68.clone | all-reduce | flops 3072 | bytes 24576
  545.8 8.2 %fusion = f32[732,6]{0,1:T(8,128)S(1)} fusion(s32[10000]{0:T(1024)S(1)} %copy-done.66, f32[6,40000]{1,0:T(8,128)S(1)} %reshape.280), kind=kOutput, calls=%fused_computation.1 | convolution fusion | flops 534360000 | bytes 382112 | tf_op jit(solution)/shard_map/hn,nr->rh/dot_general | solution.py:65
  554.0 8.4 %fusion.3 = f32[732,6]{0,1:T(8,128)S(1)} fusion(s32[10000]{0:T(1024)S(1)} %copy-done.68, f32[6,40000]{1,0:T(8,128)S(1)} %reshape.280), kind=kOutput, calls=%fused_computation.5 | convolution fusion | flops 534360000 | bytes 382112 | tf_op jit(solution)/shard_map/hn,nr->rh/dot_general | solution.py:65
  562.4 8.4 %fusion.6 = f32[732,6]{0,1:T(8,128)S(1)} fusion(s32[10000]{0:T(1024)S(1)} %copy-done.64, f32[6,40000]{1,0:T(8,128)S(1)} %reshape.280), kind=kOutput, calls=%fused_computation.9 | convolution fusion | flops 534360000 | bytes 382112 | tf_op jit(solution)/shard_map/hn,nr->rh/dot_general | solution.py:65
  570.9 8.2 %fusion.92 = f32[732,6]{0,1:T(8,128)S(1)} fusion(f32[732,6]{0,1:T(8,128)S(1)} %fusion, f32[732,6]{0,1:T(8,128)S(1)} %fusion.3, f32[732,6]{0,1:T(8,128)S(1)} %fusion.6, s32[10000]{0:T(1024)S(1)} %copy-done.62, f32[6,40000]{1,0:T(8,128)S(1)} %reshape.280), kind=kOutput, calls=%fused_computation.177 | convolution fusion | flops 534373184 | bytes 455840 | tf_op jit(solution)/shard_map/hn,nr->rh/dot_general | solution.py:65
  579.1 9.5 %fusion.89 = f32[732,6]{0,1:T(8,128)S(1)} fusion(f32[732,6]{0,1:T(8,128)S(1)} %fusion.92, f32[732,6]{0,1:T(8,128)S(1)} %fusion.1, f32[732,6]{0,1:T(8,128)S(1)} %fusion.4, f32[732,6]{0,1:T(8,128)S(1)} %fusion.7, s32[10000]{0:T(1024)S(1)} %copy-done.62, f32[6,40000]{1,0:T(8,128)} %copy-done.37), kind=kOutput, calls=%fused_computation.174 | convolution fusion | flops 534377568 | bytes 451424 | tf_op jit(solution)/shard_map/hn,nr->rh/dot_general | solution.py:65
  599.3 78.8 %all-reduce.2 = (f32[768]{0:T(1024)}, f32[768]{0:T(1024)}, f32[768]{0:T(1024)}, f32[2,384]{1,0:T(2,128)}, f32[732,6]{0,1:T(8,128)}, /*index=5*/f32[768]{0:T(1024...) all-reduce(f32[768]{0:T(1024)S(1)} %get-tuple-element.57, ...), channel_id=1, replica_groups=mesh['dp'=16,'head'=2] {'dp'}, use_global_device_ids=true, to_apply=%region_29.30 | all-reduce | flops 12072 | bytes 96576 | tf_op jit(solution)/shard_map/psum | solution.py:97
  681.4 58.1 %reduce-scatter.17.cloned.1.call-done = f32[96,768]{1,0:T(8,128)} async-done(((f32[3072,768]{1,0:T(8,128)}), f32[96,768]{1,0:T(8,128)}) %reduce-scatter.17.cloned.1.call-update) | async-done | bytes 294928 | tf_op jit(solution)/shard_map/reduce_scatter | solution.py:106
  (384 shorter events, 205.5 us)
Async XLA Ops:
  8.0 80.6 %copy-start = (bf16[768,3,384]{2,0,1:T(8,128)(2,1)S(1)}, bf16[768,3,384]{2,0,1:T(8,128)(2,1)}, u32[]{:S(2)}) copy-start(bf16[768,3,384]{2,0,1:T(8,128)(2,1)} %param.28) | copy-start | bytes 5308420
  8.1 80.5 %all-gather.7.cloned.1.call-start = ((), (), s32[]{:S(2)}) async-start(), calls=%async_computation.6 | async-start | bytes 1843200 | tf_op jit(solution)/shard_map/all_gather | solution.py:157
  9.0 305.5 %copy-start.52 = (f32[2,200]{1,0:T(2,128)}, f32[2,200]{1,0:T(2,128)S(1)}, u32[]{:S(2)}) copy-start(f32[2,200]{1,0:T(2,128)S(1)} %get-tuple-element.102) | copy-start | bytes 4804
  9.8 304.7 %copy-start.54 = (f32[2,200]{1,0:T(2,128)}, f32[2,200]{1,0:T(2,128)S(1)}, u32[]{:S(2)}) copy-start(f32[2,200]{1,0:T(2,128)S(1)} %get-tuple-element.100) | copy-start | bytes 4804
  11.2 303.3 %copy-start.56 = (f32[2,200]{1,0:T(2,128)}, f32[2,200]{1,0:T(2,128)S(1)}, u32[]{:S(2)}) copy-start(f32[2,200]{1,0:T(2,128)S(1)} %broadcast_multiply_fusion.5) | copy-start | bytes 4804
  12.9 301.6 %copy-start.71 = (f32[2,200]{1,0:T(2,128)}, f32[2,200]{1,0:T(2,128)S(1)}, u32[]{:S(2)}) copy-start(f32[2,200]{1,0:T(2,128)S(1)} %fusion.121) | copy-start | bytes 4804
  14.8 142.5 %reduce-scatter.7.cloned.1.call-start = ((), (), s32[]{:S(2)}) async-start(), calls=%async_computation.7 | async-start | bytes 3686400 | tf_op jit(solution)/shard_map/reduce_scatter | solution.py:182
  15.2 15.9 %copy-start.63 = (s32[10000]{0:T(1024)}, s32[10000]{0:T(1024)S(1)}, u32[]{:S(2)}) copy-start(s32[10000]{0:T(1024)S(1)} %eq.36) | copy-start | bytes 120004
  45.6 21.1 %copy-start.65 = (s32[10000]{0:T(1024)}, s32[10000]{0:T(1024)S(1)}, u32[]{:S(2)}) copy-start(s32[10000]{0:T(1024)S(1)} %eq.44) | copy-start | bytes 120004
  45.7 18.8 %copy-start.67 = (s32[10000]{0:T(1024)}, s32[10000]{0:T(1024)S(1)}, u32[]{:S(2)}) copy-start(s32[10000]{0:T(1024)S(1)} %eq.40) | copy-start | bytes 120004
  50.1 16.6 %copy-start.95 = (f32[732,6]{0,1:T(8,128)S(1)}, f32[732,6]{0,1:T(8,128)}, u32[]{:S(2)}) copy-start(f32[732,6]{0,1:T(8,128)} %param.30) | copy-start | bytes 52708
  112.5 44.8 %copy-start.69 = (f32[768]{0:T(1024)S(1)}, f32[768]{0:T(1024)}, u32[]{:S(2)}) copy-start(f32[768]{0:T(1024)} %param.32) | copy-start | bytes 9220
  112.5 44.8 %copy-start.70 = (f32[768]{0:T(1024)S(1)}, f32[768]{0:T(1024)}, u32[]{:S(2)}) copy-start(f32[768]{0:T(1024)} %param.33) | copy-start | bytes 9220
  112.5 70.2 %all-gather.9.cloned.1.call-start = ((), (), s32[]{:S(2)}) async-start(), calls=%async_computation.8 | async-start | bytes 4866048 | tf_op jit(solution)/shard_map/all_gather | solution.py:143
  113.1 134.6 %all-gather.11.cloned.1.call-start = ((), (), s32[]{:S(2)}) async-start(), calls=%async_computation.9 | async-start | bytes 4866048 | tf_op jit(solution)/shard_map/all_gather | solution.py:145
  113.7 155.4 %all-gather.15.cloned.1.call-start = ((), (), s32[]{:S(2)}) async-start(), calls=%async_computation.12 | async-start | bytes 1843200 | tf_op jit(solution)/shard_map/all_gather | solution.py:259
  159.1 23.6 %copy-start.51 = (f32[768]{0:T(1024)S(1)}, f32[768]{0:T(1024)}, u32[]{:S(2)}) copy-start(f32[768]{0:T(1024)} %param.34) | copy-start | bytes 9220
  159.1 23.6 %copy-start.60 = (f32[768]{0:T(1024)S(1)}, f32[768]{0:T(1024)}, u32[]{:S(2)}) copy-start(f32[768]{0:T(1024)} %param.35) | copy-start | bytes 9220
  160.4 87.3 %copy-start.87 = (f32[768]{0:T(1024)S(1)}, f32[768]{0:T(1024)}, u32[]{:S(2)}) copy-start(f32[768]{0:T(1024)} %param.40) | copy-start | bytes 9220
  261.4 50.5 %reduce-scatter.11.cloned.1.call-start = ((), (), s32[]{:S(2)}) async-start(), calls=%async_computation.13 | async-start | bytes 3686400 | tf_op jit(solution)/shard_map/reduce_scatter | solution.py:324
  300.6 28.0 %all-gather.13.cloned.1.call-start = ((), (), s32[]{:S(2)}) async-start(), calls=%async_computation.10 | async-start | bytes 1843200 | tf_op jit(solution)/shard_map/all_gather | solution.py:157
  317.9 45.8 %reduce-scatter.9.cloned.1.call-start = ((), (), s32[]{:S(2)}) async-start(), calls=%async_computation.11 | async-start | bytes 3686400 | tf_op jit(solution)/shard_map/reduce_scatter | solution.py:182
  352.4 44.8 %all-gather.17.cloned.1.call-start = ((), (), s32[]{:S(2)}) async-start(), calls=%async_computation.14 | async-start | bytes 1843200 | tf_op jit(solution)/shard_map/all_gather | solution.py:259
  365.7 16.8 %copy-start.9 = (f32[2,200,768]{2,1,0:T(8,128)}, f32[2,200,768]{2,1,0:T(8,128)S(1)}, u32[]{:S(2)}) copy-start(f32[2,200,768]{2,1,0:T(8,128)S(1)} %get-tuple-element.77) | copy-start | bytes 3686404
  386.5 202.2 %reduce-scatter.13.cloned.1.call-start = ((), (), s32[]{:S(2)}) async-start(), calls=%async_computation.15 | async-start | bytes 3686400 | tf_op jit(solution)/shard_map/reduce_scatter | solution.py:324
  428.5 252.9 %all-reduce.7.cloned.1.call-start = ((), (), s32[]{:S(2)}) async-start(), calls=%async_computation.18 | async-start | bytes 9437184 | tf_op jit(solution)/shard_map/psum | solution.py:96
  441.9 239.5 %reduce-scatter.15.cloned.1.call-start = ((), (), s32[]{:S(2)}) async-start(), calls=%async_computation.16 | async-start | bytes 9732096 | tf_op jit(solution)/shard_map/reduce_scatter | solution.py:104
  453.2 286.3 %reduce-scatter.17.cloned.1.call-start = ((), (), s32[]{:S(2)}) async-start(), calls=%async_computation.17 | async-start | bytes 9732096 | tf_op jit(solution)/shard_map/reduce_scatter | solution.py:106
  469.8 16.6 %copy-start.37 = (f32[6,40000]{1,0:T(8,128)}, f32[6,40000]{1,0:T(8,128)S(1)}, u32[]{:S(2)}) copy-start(f32[6,40000]{1,0:T(8,128)S(1)} %reshape.279) | copy-start | bytes 2880004
  486.4 53.1 %copy-start.88 = (f32[768]{0:T(1024)S(1)}, f32[768]{0:T(1024)}, u32[]{:S(2)}) copy-start(f32[768]{0:T(1024)} %get-tuple-element.37) | copy-start | bytes 9220
  486.4 53.1 %copy-start.81 = (f32[768]{0:T(1024)S(1)}, f32[768]{0:T(1024)}, u32[]{:S(2)}) copy-start(f32[768]{0:T(1024)} %get-tuple-element.24) | copy-start | bytes 9220
  486.4 53.1 %copy-start.83 = (f32[768]{0:T(1024)S(1)}, f32[768]{0:T(1024)}, u32[]{:S(2)}) copy-start(f32[768]{0:T(1024)} %get-tuple-element.73) | copy-start | bytes 9220
  (89 other events, 421.2 us)
Sparse Core Ops, SparseCore 0:
  14.9 11.9 all-gather.6
  112.6 12.7 reduce-scatter.6
  261.5 7.5 all-gather.14
  300.7 11.1 reduce-scatter.10
  318.0 10.5 all-gather.12
  352.5 11.1 reduce-scatter.8
  386.6 10.5 all-gather.16
  428.6 11.1 reduce-scatter.12
  453.3 145.3 reduce-scatter.14
  605.1 134.3 reduce-scatter.16
Sparse Core Ops, SparseCore 1:
  115.9 66.7 all-gather.8
  185.5 62.1 all-gather.10
  442.0 201.9 all-reduce.6
